TPU v7x, 256 devices: a whole 4x4x8 slice. The times are simulated.
256 devices in a mesh: group: 16 (over z, core), dev: 16 (over y, x).
Axes of the slice: x: 4, y: 4, z: 8, core: 2. Of those that a mesh axis runs over, the one named last changes fastest.
Arguments:
- tokens: bfloat16 [1024, 7168], P(('group', 'dev')), may hold values from -6 to 6
- group_ids: int32 [1024, 4], P(('group', 'dev')), may hold values from 0 to 15, as said below
- expert_ids: int32 [1024, 8], P(('group', 'dev')), may hold values from 0 to 63, as said below
- gate_scores: bfloat16 [1024, 8], P(('group', 'dev')), may hold values from 0.099609375 to 1
- w_gate: bfloat16 [7168, 65536], P(None, ('group', 'dev')), may hold values from -0.0625 to 0.0625
- w_up: bfloat16 [7168, 65536], P(None, ('group', 'dev')), may hold values from -0.0625 to 0.0625
- w_down: bfloat16 [65536, 7168], P(('group', 'dev')), may hold values from -0.1875 to 0.1875
Outputs:
- combined: bfloat16 [1024, 7168], P(('group', 'dev'))
Inputs may be any that keep to these rules, and one draw needn't show every extreme that they name: `group_ids`: each row names 4 different groups; among the 4 rows of one aligned block, at most 2 rows name any one group. `expert_ids`: each row names 8 different experts, exactly two in each group of the row's group_ids (expert x lies in group x // 4).
All inputs are finite; a program needn't handle non-finite values.
Results may differ from a plain program's by a relative error of at most 0.014.
Values may be sent and summed in bfloat16 or wider, within the bound.
No kernel may reach another device: no remote copies, remote signals or barrier semaphores. Data moves between devices by JAX's collectives and lax.ppermute only.
A program may use at most 64 MiB of HBM per device.

v0:
```python
import jax
import jax.numpy as jnp
from jax import lax
from jax.sharding import PartitionSpec as P

FF = 1024
EXP_GROUP = 4
CAP = 2


def local(tokens, group_ids, expert_ids, gate_scores, w_gate, w_up, w_down):
    group_count = lax.axis_size("group")
    dev_count = lax.axis_size("dev")
    model_width = tokens.shape[1]
    block_cols = w_gate.shape[1]
    expert_total = group_count * EXP_GROUP
    group_iota = jnp.arange(group_count, dtype=jnp.int32)
    member = jnp.sum((group_ids[:, :, None] == group_iota[None, None, :]).astype(jnp.int32), axis=1)
    before = jnp.cumsum(member, axis=0) - member
    slot_iota = jnp.arange(CAP, dtype=jnp.int32)
    select = (member.T[:, None, :] == 1) & (before.T[:, None, :] == slot_iota[None, :, None])
    select_rows = select.astype(jnp.bfloat16)
    matches = (
        expert_ids[:, :, None] == jnp.arange(expert_total, dtype=jnp.int32)[None, None, :]
    ).astype(jnp.float32)
    coef = jnp.sum(gate_scores.astype(jnp.float32)[:, :, None] * matches, axis=1)
    coef = coef.reshape(-1, group_count, EXP_GROUP).astype(jnp.bfloat16)
    send_rows = jnp.einsum(
        "gst,td->gsd", select_rows, tokens, preferred_element_type=jnp.float32
    ).astype(jnp.bfloat16)
    send_coef = jnp.einsum(
        "gst,tge->gse", select_rows, coef, preferred_element_type=jnp.float32
    ).astype(jnp.bfloat16)
    recv_rows, recv_coef = (
        lax.all_to_all(send_rows, "group", split_axis=0, concat_axis=0, tiled=True),
        lax.all_to_all(send_coef, "group", split_axis=0, concat_axis=0, tiled=True),
    )
    all_rows, all_coef = (
        lax.all_gather(recv_rows, "dev", axis=0, tiled=True),
        lax.all_gather(recv_coef, "dev", axis=0, tiled=True),
    )
    flat_rows = all_rows.reshape(-1, model_width)
    flat_coef = all_coef.reshape(-1, EXP_GROUP)
    dev_index = lax.axis_index("dev")
    owner_expert = (dev_index * block_cols + jnp.arange(block_cols, dtype=jnp.int32)) // FF
    onehot = (owner_expert[None, :] == jnp.arange(EXP_GROUP, dtype=jnp.int32)[:, None]).astype(
        jnp.bfloat16
    )
    gate_out = jnp.dot(flat_rows, w_gate, preferred_element_type=jnp.float32)
    up_out = jnp.dot(flat_rows, w_up, preferred_element_type=jnp.float32)
    col_scale = jnp.dot(flat_coef, onehot, preferred_element_type=jnp.float32)
    hidden = (col_scale * jax.nn.silu(gate_out) * up_out).astype(jnp.bfloat16)
    partial_value = lax.optimization_barrier(
        jnp.dot(hidden, w_down, preferred_element_type=jnp.float32).astype(jnp.bfloat16)
    )
    partial_value = partial_value.reshape(dev_count, group_count, CAP, model_width)
    moved_back = lax.all_to_all(partial_value, "group", split_axis=1, concat_axis=1, tiled=True)
    summed = lax.psum_scatter(
        moved_back.astype(jnp.float32).astype(jnp.bfloat16), "dev", scatter_dimension=0, tiled=True
    )
    returned = summed.reshape(group_count, CAP, model_width)
    combined = jnp.einsum("gst,gsd->td", select_rows, returned, preferred_element_type=jnp.float32)
    return combined.astype(jnp.bfloat16)


def solution(mesh):
    return jax.shard_map(
        local,
        mesh=mesh,
        in_specs=(
            P(("group", "dev"), None),
            P(("group", "dev"), None),
            P(("group", "dev"), None),
            P(("group", "dev"), None),
            P(None, ("group", "dev")),
            P(None, ("group", "dev")),
            P(("group", "dev"), None),
        ),
        out_specs=P(("group", "dev"), None),
        check_vma=False,
    )
```

profile of v0, /device:TPU:2, one launch (start us, length us, event | category | flops | bytes accessed | tf_op | source)
XLA Modules:
  0.0 424.0 jit_solution(7251178532512982187)
XLA Ops:
  6.5 0.8 convert_reduce_fusion
  7.4 0.4 convolution_convert_fusion.1
  7.8 0.5 copy.26
  8.2 23.2 %all_to_all.15 = bf16[16,2,7168]{2,1,0:T(2,128)(2,1)} all-to-all(bf16[16,2,7168]{2,1,0:T(2,128)(2,1)S(1)} %copy.26), channel_id=1, replica_groups=mesh['group'=16,'dev'=16] {'group'}, dimensions={0} | all-to-all | bytes 917504 | tf_op jit(solution)/shard_map/all_to_all | solution.py:35
  31.5 0.1 copy.24
  31.6 0.7 convert_element_type.33
  32.3 0.8 select_reduce_fusion
  33.1 0.1 convert_element_type.35
  33.2 0.8 convolution_convert_fusion.2
  33.9 4.0 all-to-all-start
  38.0 7.5 %all-to-all-done = bf16[16,2,4]{2,1,0:T(2,128)(2,1)S(1)} async-done(((bf16[16,2,4]{2,1,0:T(2,128)(2,1)}), bf16[16,2,4]{2,1,0:T(2,128)(2,1)S(1)}, u32[]{:S(2)}, u32[]{:S(2)}) %all-to-all-start) | async-done | bytes 288 | tf_op jit(solution)/shard_map/all_to_all | solution.py:36
  45.5 23.8 %all_gather.6 = bf16[256,2,4]{2,1,0:T(2,128)(2,1)S(1)} all-gather(bf16[16,2,4]{2,1,0:T(2,128)(2,1)S(1)} %all-to-all-done), channel_id=1, replica_groups=mesh['group'=16,'dev'=16] {'dev'}, dimensions={0}, use_global_device_ids=true | all-gather | bytes 4352 | tf_op jit(solution)/shard_map/all_gather | solution.py:40
  69.3 32.0 %all-gather.2.cloned.1.call-done = bf16[256,2,7168]{2,1,0:T(2,128)(2,1)} async-done(((bf16[16,2,7168]{2,1,0:T(2,128)(2,1)}), bf16[256,2,7168]{2,1,0:T(2,128)(2,1)}) %all-gather.2.cloned.1.call-update) | async-done | bytes 7340048 | tf_op jit(solution)/shard_map/all_gather | solution.py:39
  101.3 15.4 %reshape.40 = bf16[512,7168]{1,0:T(8,128)(2,1)} reshape(bf16[256,2,7168]{2,1,0:T(2,128)(2,1)} %all-gather.2.cloned.1.call-done) | data formatting | bytes 14680064 | tf_op jit(solution)/shard_map/reshape | solution.py:42
  116.7 6.3 %fusion.16 = f32[512,256]{1,0:T(8,128)S(1)} fusion(bf16[512,7168]{1,0:T(8,128)(2,1)} %reshape.40, bf16[7168,256]{1,0:T(8,128)(2,1)} %param.11), kind=kOutput, calls=%fused_computation.32 | convolution fusion | flops 1879048192 | bytes 11534336 | tf_op jit(solution)/shard_map/dot_general | solution.py:49
  123.1 0.9 copy-done.2
  124.0 2.1 fusion.17
  126.0 6.4 %convolution_convert_fusion = bf16[512,7168]{1,0:T(8,128)(2,1)} fusion(bf16[256,7168]{1,0:T(8,128)(2,1)} %param.13, f32[512,256]{1,0:T(8,128)S(1)} %fusion.17, bf16[512,4]{1,0:T(8,128)(2,1)S(1)} %bitcast.25, f32[512,256]{1,0:T(8,128)S(1)} %fusion.16, s32[256]{0:T(256)S(1)} %and_select_fusion), kind=kOutput, calls=%fused_computation | convolution fusion | flops 1884685312 | bytes 12063744 | tf_op jit(solution)/shard_map/dot_general | solution.py:54
  132.4 14.9 %reshape.41 = bf16[16,16,2,7168]{3,2,1,0:T(2,128)(2,1)} reshape(bf16[512,7168]{1,0:T(8,128)(2,1)} %convolution_convert_fusion) | data formatting | bytes 14680064 | tf_op jit(solution)/shard_map/reshape | solution.py:56
  147.3 6.6 %copy.27 = bf16[16,16,2,7168]{3,2,0,1:T(2,128)(2,1)S(1)} copy(bf16[16,16,2,7168]{3,2,1,0:T(2,128)(2,1)} %reshape.41) | data formatting | bytes 14680064 | tf_op jit(solution)/shard_map/reshape | solution.py:56
  153.9 168.9 %all_to_all.16 = bf16[16,16,2,7168]{3,2,0,1:T(2,128)(2,1)S(1)} all-to-all(bf16[16,16,2,7168]{3,2,0,1:T(2,128)(2,1)S(1)} %copy.27), channel_id=1, replica_groups=mesh['group'=16,'dev'=16] {'group'}, dimensions={1} | all-to-all | bytes 14680064 | tf_op jit(solution)/shard_map/all_to_all | solution.py:57
  322.8 7.0 %copy.28 = bf16[16,16,2,7168]{3,1,2,0:T(8,128)(2,1)} copy(bf16[16,16,2,7168]{3,2,0,1:T(2,128)(2,1)S(1)} %all_to_all.16) | data formatting | bytes 14680064 | tf_op jit(solution)/shard_map/all_to_all | solution.py:57
  329.8 85.4 %reduce-scatter.4.cloned.1.call-done = bf16[1,16,2,7168]{3,1,2,0:T(8,128)(2,1)} async-done(((bf16[16,16,2,7168]{3,1,2,0:T(8,128)(2,1)}), bf16[1,16,2,7168]{3,1,2,0:T(8,128)(2,1)}) %reduce-scatter.4.cloned.1.call-update) | async-done | bytes 458768
  415.2 1.9 fusion
  (14 shorter events, 0.2 us)
Async XLA Ops:
  6.5 0.9 copy-start
  6.5 94.7 %all-gather.2.cloned.1.call-start = ((), (), s32[]{:S(2)}) async-start(), calls=%async_computation.4 | async-start | bytes 7798784 | tf_op jit(solution)/shard_map/all_gather | solution.py:39
  33.9 11.5 %all-to-all-start = ((bf16[16,2,4]{2,1,0:T(2,128)(2,1)}), bf16[16,2,4]{2,1,0:T(2,128)(2,1)S(1)}, u32[]{:S(2)}, u32[]{:S(2)}) async-start(bf16[16,2,4]{2,1,0:T(2,128)(2,1)} %convolution_convert_fusion.2), calls=%async_computation | async-start | bytes 16384 | tf_op jit(solution)/shard_map/all_to_all | solution.py:36
  38.0 377.3 %reduce-scatter.4.cloned.1.call-start = ((), (), s32[]{:S(2)}) async-start(), calls=%async_computation.5 | async-start | bytes 7798784
  116.7 6.3 %copy-start.1 = (bf16[512,7168]{1,0:T(8,128)(2,1)S(1)}, bf16[512,7168]{1,0:T(8,128)(2,1)}, u32[]{:S(2)}) copy-start(bf16[512,7168]{1,0:T(8,128)(2,1)} %reshape.40) | copy-start | bytes 22020100
  116.7 7.3 %copy-start.2 = (bf16[7168,256]{1,0:T(8,128)(2,1)S(1)}, bf16[7168,256]{1,0:T(8,128)(2,1)}, u32[]{:S(2)}) copy-start(bf16[7168,256]{1,0:T(8,128)(2,1)} %param.12) | copy-start | bytes 11010052
Sparse Core Ops, SparseCore 0:
  31.6 69.5 all-gather.1
  330.0 85.2 reduce-scatter.3
where the time goes:
time: 425 us; the launch traced here: 424 us
  blocking collectives  216 us (51%)
  waiting for transfers between devices  125 us (29%)
  local copies, waits for them, and re-layouts  45.5 us (11%)
  matrix products  17.8 us (4%)
  between operations  13.5 us (3%)
    all_to_all x1, blocking collectives, local(): lax.all_to_all(partial_value, 'group', split_axis=1, concat_axis=1, tiled...  169 us
    unnamed x3, waiting for transfers between devices  85.4 us
    all_gather x1, waiting for transfers between devices, local(): lax.all_gather(recv_rows, 'dev', axis=0, tiled=True)  32 us
    all_gather x1, blocking collectives, local(): lax.all_gather(recv_coef, 'dev', axis=0, tiled=True)  23.8 us
    all_to_all x1, blocking collectives, local(): lax.all_to_all(send_rows, 'group', split_axis=0, concat_axis=0, tiled=True)  23.2 us
    reshape x2, local copies, waits for them, and re-layouts, local(): partial_value.reshape(dev_count, group_count, CAP, model_width)  21.5 us
    reshape x1, local copies, waits for them, and re-layouts, local(): flat_rows = all_rows.reshape(-1, model_width)  15.4 us
  transfers between devices with their start and end apart: 3, of which 3 were waited for; matrix products, arithmetic and copies ran while one was open for 1% of the time, Pallas kernels for 0%

commit v1 on v0

--- a/solution.py
+++ b/solution.py
@@ -6,6 +6,22 @@
 FF = 1024
 EXP_GROUP = 4
 CAP = 2
+
+
+def collect(x, axis, dim):
+    ways, here, turn = (lax.axis_size(axis), lax.axis_index(axis), x.shape[dim])
+    lengths = [n * ways if d == dim else n for d, n in enumerate(x.shape)]
+    full = lax.dynamic_update_slice_in_dim(jnp.zeros(lengths, x.dtype), x, here * turn, axis=dim)
+    going_up = going_down = x
+    for far in range(1, ways // 2 + 1):
+        going_up = lax.ppermute(going_up, axis, [(d, (d + 1) % ways) for d in range(ways)])
+        full = lax.dynamic_update_slice_in_dim(full, going_up, (here - far) % ways * turn, axis=dim)
+        if 2 * far < ways:
+            going_down = lax.ppermute(going_down, axis, [(d, (d - 1) % ways) for d in range(ways)])
+            full = lax.dynamic_update_slice_in_dim(
+                full, going_down, (here + far) % ways * turn, axis=dim
+            )
+    return full
 
 
 def local(tokens, group_ids, expert_ids, gate_scores, w_gate, w_up, w_down):
@@ -36,7 +52,7 @@
         lax.all_to_all(send_coef, "group", split_axis=0, concat_axis=0, tiled=True),
     )
     all_rows, all_coef = (
-        lax.all_gather(recv_rows, "dev", axis=0, tiled=True),
+        collect(recv_rows, "dev", 0),
         lax.all_gather(recv_coef, "dev", axis=0, tiled=True),
     )
     flat_rows = all_rows.reshape(-1, model_width)

time: 425 us -> 495 us (1.16)
  starting transfers between devices: 4.05 us -> 39 us
  waiting for transfers between devices: 125 us -> 152 us
  local copies, waits for them, and re-layouts: 45.5 us -> 67.9 us
  blocking collectives: 216 us -> 194 us
  matrix products: 17.8 us -> 25.4 us
    ppermute x0 -> x15, waiting for transfers between devices: none -> 59.2 us  [the longest x8 58.7 us: collect(): lax.ppermute(going_up, axis, [(d, (d + 1) % ways) for d in range(ways)])]
    all_gather x1 -> x0, waiting for transfers between devices: 32 us -> none  [local(): lax.all_gather(recv_rows, 'dev', axis=0, tiled=True)]
    ppermute x0 -> x15, starting transfers between devices: none -> 26.8 us  [the longest x7 15.5 us: collect(): lax.ppermute(going_down, axis, [(d, (d - 1) % ways) for d in range(ways)])]
    all_to_all x1 -> x0, blocking collectives: 23.2 us -> none  [local(): lax.all_to_all(send_rows, 'group', split_axis=0, concat_axis=0, tiled=True)]
    dynamic_update_slice x0 -> x16, local copies, waits for them, and re-layouts: none -> 17.7 us  [the longest x8 8.77 us: collect(): lax.dynamic_update_slice_in_dim(full, going_up, (here - far) % ways * tur...]
    dot_general x1, matrix products: 6.38 us -> 16 us  [local(): jnp.dot(hidden, w_down, preferred_element_type=jnp.float32)]
    unnamed x3 -> x2, waiting for transfers between devices: 85.4 us -> 87.1 us
  transfers between devices with their start and end apart: 3 -> 18, of which waited for: 3 -> 13; matrix products, arithmetic and copies ran while one was open for 1% -> 5% of each run, Pallas kernels for 0% -> 0%
where the time goes in v1:
time: 495 us; the launch traced here: 494 us
  blocking collectives  194 us (39%)
  waiting for transfers between devices  152 us (31%)
  local copies, waits for them, and re-layouts  67.9 us (14%)
  starting transfers between devices  39 us (8%)
  matrix products  25.4 us (5%)
  between operations  13.8 us (3%)
    all_to_all x1, blocking collectives, local(): lax.all_to_all(partial_value, 'group', split_axis=1, concat_axis=1, tiled...  170 us
    unnamed x2, waiting for transfers between devices  87.1 us
    ppermute x8, waiting for transfers between devices, collect(): lax.ppermute(going_up, axis, [(d, (d + 1) % ways) for d in range(ways)])  58.7 us
    all_gather x1, blocking collectives, local(): lax.all_gather(recv_coef, 'dev', axis=0, tiled=True)  23.8 us
    reshape x2, local copies, waits for them, and re-layouts, local(): partial_value.reshape(dev_count, group_count, CAP, model_width)  21.5 us
    dot_general x1, matrix products, local(): jnp.dot(hidden, w_down, preferred_element_type=jnp.float32)  16 us
    ppermute x7, starting transfers between devices, collect(): lax.ppermute(going_down, axis, [(d, (d - 1) % ways) for d in range(ways)])  15.5 us
    reshape x1, local copies, waits for them, and re-layouts, local(): flat_rows = all_rows.reshape(-1, model_width)  15.4 us
  transfers between devices with their start and end apart: 18, of which 13 were waited for; matrix products, arithmetic and copies ran while one was open for 5% of the time, Pallas kernels for 0%

profile of v1, /device:TPU:2, one launch (start us, length us, event | category | flops | bytes accessed | tf_op | source)
XLA Modules:
  0.0 494.3 jit_solution(18079745717984911997)
XLA Ops:
  9.8 8.6 %all-to-all-start = ((bf16[16,2,4]{2,1,0:T(2,128)(2,1)}), bf16[16,2,4]{2,1,0:T(2,128)(2,1)S(1)}, u32[]{:S(2)}, u32[]{:S(2)}) async-start(bf16[16,2,4]{2,1,0:T(2,128)(2,1)} %convolution_convert_fusion.2), calls=%async_computation | async-start | bytes 16384 | tf_op jit(solution)/shard_map/all_to_all | solution.py:52
  20.0 5.9 %all-to-all-done = bf16[16,2,4]{2,1,0:T(2,128)(2,1)S(1)} async-done(((bf16[16,2,4]{2,1,0:T(2,128)(2,1)}), bf16[16,2,4]{2,1,0:T(2,128)(2,1)S(1)}, u32[]{:S(2)}, u32[]{:S(2)}) %all-to-all-start) | async-done | bytes 288 | tf_op jit(solution)/shard_map/all_to_all | solution.py:52
  25.9 3.6 all-to-all-start.1
  29.8 23.8 %all_gather.3 = bf16[256,2,4]{2,1,0:T(2,128)(2,1)S(1)} all-gather(bf16[16,2,4]{2,1,0:T(2,128)(2,1)S(1)} %all-to-all-done), channel_id=1, replica_groups=mesh['group'=16,'dev'=16] {'dev'}, dimensions={0}, use_global_device_ids=true | all-gather | bytes 4352 | tf_op jit(solution)/shard_map/all_gather | solution.py:56
  56.0 4.9 broadcast_in_dim.2
  64.0 2.5 collective-permute-start.2
  68.8 7.5 %collective-permute-done.2 = bf16[16,2,7168]{2,1,0:T(2,128)(2,1)S(1)} collective-permute-done((bf16[16,2,7168]{2,1,0:T(2,128)(2,1)S(1)}, bf16[16,2,7168]{2,1,0:T(2,128)(2,1)S(1)}, u32[]{:S(2)}, u32[]{:S(2)}) %collective-permute-start.2) | collective-permute-done | bytes 458784 | tf_op jit(solution)/shard_map/ppermute | solution.py:17
  81.1 8.5 %collective-permute-done.4 = bf16[16,2,7168]{2,1,0:T(2,128)(2,1)S(1)} collective-permute-done((bf16[16,2,7168]{2,1,0:T(2,128)(2,1)S(1)}, bf16[16,2,7168]{2,1,0:T(2,128)(2,1)S(1)}, u32[]{:S(2)}, u32[]{:S(2)}) %collective-permute-start.4) | collective-permute-done | bytes 458784 | tf_op jit(solution)/shard_map/ppermute | solution.py:17
  94.6 7.5 %collective-permute-done.6 = bf16[16,2,7168]{2,1,0:T(2,128)(2,1)S(1)} collective-permute-done((bf16[16,2,7168]{2,1,0:T(2,128)(2,1)S(1)}, bf16[16,2,7168]{2,1,0:T(2,128)(2,1)S(1)}, u32[]{:S(2)}, u32[]{:S(2)}) %collective-permute-start.6) | collective-permute-done | bytes 458784 | tf_op jit(solution)/shard_map/ppermute | solution.py:17
  104.6 2.7 collective-permute-start.9
  109.5 7.6 %collective-permute-done.8 = bf16[16,2,7168]{2,1,0:T(2,128)(2,1)S(1)} collective-permute-done((bf16[16,2,7168]{2,1,0:T(2,128)(2,1)S(1)}, bf16[16,2,7168]{2,1,0:T(2,128)(2,1)S(1)}, u32[]{:S(2)}, u32[]{:S(2)}) %collective-permute-start.8) | collective-permute-done | bytes 458784 | tf_op jit(solution)/shard_map/ppermute | solution.py:17
  117.3 6.1 %collective-permute-start.11 = (bf16[16,2,7168]{2,1,0:T(2,128)(2,1)S(1)}, bf16[16,2,7168]{2,1,0:T(2,128)(2,1)S(1)}, u32[]{:S(2)}, u32[]{:S(2)}) collective-permute-start(bf16[16,2,7168]{2,1,0:T(2,128)(2,1)S(1)} %collective-permute-done.9), channel_id=1, source_target_pairs={{0,15},{1,0},{2,1},{3,2},{4,3},{5,4},{6,5},{7,6},{8,7},{9,8},{10,9... | collective-permute-start | bytes 1376264 | tf_op jit(solution)/shard_map/ppermute | solution.py:20
  125.7 8.4 %collective-permute-done.10 = bf16[16,2,7168]{2,1,0:T(2,128)(2,1)S(1)} collective-permute-done((bf16[16,2,7168]{2,1,0:T(2,128)(2,1)S(1)}, bf16[16,2,7168]{2,1,0:T(2,128)(2,1)S(1)}, u32[]{:S(2)}, u32[]{:S(2)}) %collective-permute-start.10) | collective-permute-done | bytes 458784 | tf_op jit(solution)/shard_map/ppermute | solution.py:17
  134.1 5.5 %collective-permute-start.13 = (bf16[16,2,7168]{2,1,0:T(2,128)(2,1)S(1)}, bf16[16,2,7168]{2,1,0:T(2,128)(2,1)S(1)}, u32[]{:S(2)}, u32[]{:S(2)}) collective-permute-start(bf16[16,2,7168]{2,1,0:T(2,128)(2,1)S(1)} %collective-permute-done.11), channel_id=1, source_target_pairs={{0,15},{1,0},{2,1},{3,2},{4,3},{5,4},{6,5},{7,6},{8,7},{9,8},{10,9... | collective-permute-start | bytes 1376264 | tf_op jit(solution)/shard_map/ppermute | solution.py:20
  141.9 8.0 %collective-permute-done.12 = bf16[16,2,7168]{2,1,0:T(2,128)(2,1)S(1)} collective-permute-done((bf16[16,2,7168]{2,1,0:T(2,128)(2,1)S(1)}, bf16[16,2,7168]{2,1,0:T(2,128)(2,1)S(1)}, u32[]{:S(2)}, u32[]{:S(2)}) %collective-permute-start.12) | collective-permute-done | bytes 458784 | tf_op jit(solution)/shard_map/ppermute | solution.py:17
  152.0 9.3 %collective-permute-done.14 = bf16[16,2,7168]{2,1,0:T(2,128)(2,1)S(1)} collective-permute-done((bf16[16,2,7168]{2,1,0:T(2,128)(2,1)S(1)}, bf16[16,2,7168]{2,1,0:T(2,128)(2,1)S(1)}, u32[]{:S(2)}, u32[]{:S(2)}) %collective-permute-start.14) | collective-permute-done | bytes 458784 | tf_op jit(solution)/shard_map/ppermute | solution.py:17
  162.4 15.4 %reshape.40 = bf16[512,7168]{1,0:T(8,128)(2,1)} reshape(bf16[256,2,7168]{2,1,0:T(2,128)(2,1)} %constant_dynamic-update-slice_fusion) | data formatting | bytes 14680064 | tf_op jit(solution)/shard_map/reshape | solution.py:58
  177.8 6.2 %fusion.16 = f32[512,256]{1,0:T(8,128)S(1)} fusion(bf16[512,7168]{1,0:T(8,128)(2,1)} %reshape.40, bf16[7168,256]{1,0:T(8,128)(2,1)} %param.11), kind=kOutput, calls=%fused_computation.49 | convolution fusion | flops 1879048192 | bytes 11534336 | tf_op jit(solution)/shard_map/dot_general | solution.py:65
  184.0 16.0 %convolution_convert_fusion = bf16[512,7168]{1,0:T(8,128)(2,1)} fusion(bf16[256,7168]{1,0:T(8,128)(2,1)} %param.13, bf16[512,7168]{1,0:T(8,128)(2,1)} %reshape.40, bf16[7168,256]{1,0:T(8,128)(2,1)} %param.12, f32[512,256]{1,0:T(8,128)S(1)} %fusion.13, f32[512,256]{1,0:T(8,128)S(1)} %fusion.16), kind=kOutput, calls=%fused_computation | convolution fusion | flops 3762683904 | bytes 23068672 | tf_op jit(solution)/shard_map/dot_general | solution.py:70
  200.0 14.9 %reshape.41 = bf16[16,16,2,7168]{3,2,1,0:T(2,128)(2,1)} reshape(bf16[512,7168]{1,0:T(8,128)(2,1)} %convolution_convert_fusion) | data formatting | bytes 14680064 | tf_op jit(solution)/shard_map/reshape | solution.py:72
  214.9 6.6 %copy.37 = bf16[16,16,2,7168]{3,2,0,1:T(2,128)(2,1)S(1)} copy(bf16[16,16,2,7168]{3,2,1,0:T(2,128)(2,1)} %reshape.41) | data formatting | bytes 14680064 | tf_op jit(solution)/shard_map/reshape | solution.py:72
  221.5 170.0 %all_to_all.15 = bf16[16,16,2,7168]{3,2,0,1:T(2,128)(2,1)S(1)} all-to-all(bf16[16,16,2,7168]{3,2,0,1:T(2,128)(2,1)S(1)} %copy.37), channel_id=1, replica_groups=mesh['group'=16,'dev'=16] {'group'}, dimensions={1} | all-to-all | bytes 14680064 | tf_op jit(solution)/shard_map/all_to_all | solution.py:73
  391.5 7.0 %copy.38 = bf16[16,16,2,7168]{3,1,2,0:T(8,128)(2,1)} copy(bf16[16,16,2,7168]{3,2,0,1:T(2,128)(2,1)S(1)} %all_to_all.15) | data formatting | bytes 14680064 | tf_op jit(solution)/shard_map/all_to_all | solution.py:73
  398.5 87.0 %reduce-scatter.4.cloned.1.call-done = bf16[1,16,2,7168]{3,1,2,0:T(8,128)(2,1)} async-done(((bf16[16,16,2,7168]{3,1,2,0:T(8,128)(2,1)}), bf16[1,16,2,7168]{3,1,2,0:T(8,128)(2,1)}) %reduce-scatter.4.cloned.1.call-update) | async-done | bytes 458768
  (57 shorter events, 37.1 us)
Async XLA Ops:
  6.5 11.8 %copy-start = (bf16[4,7168]{1,0:T(4,128)(2,1)S(1)}, bf16[4,7168]{1,0:T(4,128)(2,1)}, u32[]{:S(2)}) copy-start(bf16[4,7168]{1,0:T(4,128)(2,1)} %param.7) | copy-start | bytes 172036
  9.8 16.1 %all-to-all-start = ((bf16[16,2,4]{2,1,0:T(2,128)(2,1)}), bf16[16,2,4]{2,1,0:T(2,128)(2,1)S(1)}, u32[]{:S(2)}, u32[]{:S(2)}) async-start(bf16[16,2,4]{2,1,0:T(2,128)(2,1)} %convolution_convert_fusion.2), calls=%async_computation | async-start | bytes 16384 | tf_op jit(solution)/shard_map/all_to_all | solution.py:52
  25.9 27.9 %all-to-all-start.1 = ((bf16[16,2,7168]{2,1,0:T(2,128)(2,1)}), bf16[16,2,7168]{2,1,0:T(2,128)(2,1)S(1)}, u32[]{:S(2)}, u32[]{:S(2)}) async-start(bf16[16,2,7168]{2,1,0:T(2,128)(2,1)} %copy.36), calls=%async_computation.1 | async-start | bytes 917504 | tf_op jit(solution)/shard_map/all_to_all | solution.py:51
  29.5 456.1 %reduce-scatter.4.cloned.1.call-start = ((), (), s32[]{:S(2)}) async-start(), calls=%async_computation.4 | async-start | bytes 7798784
  53.9 10.1 %collective-permute-start = (bf16[16,2,7168]{2,1,0:T(2,128)(2,1)S(1)}, bf16[16,2,7168]{2,1,0:T(2,128)(2,1)S(1)}, u32[]{:S(2)}, u32[]{:S(2)}) collective-permute-start(bf16[16,2,7168]{2,1,0:T(2,128)(2,1)S(1)} %all-to-all-done.1), channel_id=1, source_target_pairs={{0,1},{1,2},{2,3},{3,4},{4,5},{5,6},{6,7},{7,8},{8,9},{9,10},{10,1... | collective-permute-start | bytes 1376264 | tf_op jit(solution)/shard_map/ppermute | solution.py:17
  55.3 11.3 %collective-permute-start.1 = (bf16[16,2,7168]{2,1,0:T(2,128)(2,1)S(1)}, bf16[16,2,7168]{2,1,0:T(2,128)(2,1)S(1)}, u32[]{:S(2)}, u32[]{:S(2)}) collective-permute-start(bf16[16,2,7168]{2,1,0:T(2,128)(2,1)S(1)} %all-to-all-done.1), channel_id=1, source_target_pairs={{0,15},{1,0},{2,1},{3,2},{4,3},{5,4},{6,5},{7,6},{8,7},{9,8},{10,9... | collective-permute-start | bytes 1376264 | tf_op jit(solution)/shard_map/ppermute | solution.py:20
  64.0 12.3 %collective-permute-start.2 = (bf16[16,2,7168]{2,1,0:T(2,128)(2,1)S(1)}, bf16[16,2,7168]{2,1,0:T(2,128)(2,1)S(1)}, u32[]{:S(2)}, u32[]{:S(2)}) collective-permute-start(bf16[16,2,7168]{2,1,0:T(2,128)(2,1)S(1)} %collective-permute-done), channel_id=1, source_target_pairs={{0,1},{1,2},{2,3},{3,4},{4,5},{5,6},{6,7},{7,8},{8,9},{9,10},{10,1... | collective-permute-start | bytes 1376264 | tf_op jit(solution)/shard_map/ppermute | solution.py:17
  66.6 12.2 %collective-permute-start.3 = (bf16[16,2,7168]{2,1,0:T(2,128)(2,1)S(1)}, bf16[16,2,7168]{2,1,0:T(2,128)(2,1)S(1)}, u32[]{:S(2)}, u32[]{:S(2)}) collective-permute-start(bf16[16,2,7168]{2,1,0:T(2,128)(2,1)S(1)} %collective-permute-done.1), channel_id=1, source_target_pairs={{0,15},{1,0},{2,1},{3,2},{4,3},{5,4},{6,5},{7,6},{8,7},{9,8},{10,9... | collective-permute-start | bytes 1376264 | tf_op jit(solution)/shard_map/ppermute | solution.py:20
  76.3 13.3 %collective-permute-start.4 = (bf16[16,2,7168]{2,1,0:T(2,128)(2,1)S(1)}, bf16[16,2,7168]{2,1,0:T(2,128)(2,1)S(1)}, u32[]{:S(2)}, u32[]{:S(2)}) collective-permute-start(bf16[16,2,7168]{2,1,0:T(2,128)(2,1)S(1)} %collective-permute-done.2), channel_id=1, source_target_pairs={{0,1},{1,2},{2,3},{3,4},{4,5},{5,6},{6,7},{7,8},{8,9},{9,10},{10,1... | collective-permute-start | bytes 1376264 | tf_op jit(solution)/shard_map/ppermute | solution.py:17
  78.7 13.3 %collective-permute-start.5 = (bf16[16,2,7168]{2,1,0:T(2,128)(2,1)S(1)}, bf16[16,2,7168]{2,1,0:T(2,128)(2,1)S(1)}, u32[]{:S(2)}, u32[]{:S(2)}) collective-permute-start(bf16[16,2,7168]{2,1,0:T(2,128)(2,1)S(1)} %collective-permute-done.3), channel_id=1, source_target_pairs={{0,15},{1,0},{2,1},{3,2},{4,3},{5,4},{6,5},{7,6},{8,7},{9,8},{10,9... | collective-permute-start | bytes 1376264 | tf_op jit(solution)/shard_map/ppermute | solution.py:20
  89.6 12.5 %collective-permute-start.6 = (bf16[16,2,7168]{2,1,0:T(2,128)(2,1)S(1)}, bf16[16,2,7168]{2,1,0:T(2,128)(2,1)S(1)}, u32[]{:S(2)}, u32[]{:S(2)}) collective-permute-start(bf16[16,2,7168]{2,1,0:T(2,128)(2,1)S(1)} %collective-permute-done.4), channel_id=1, source_target_pairs={{0,1},{1,2},{2,3},{3,4},{4,5},{5,6},{6,7},{7,8},{8,9},{9,10},{10,1... | collective-permute-start | bytes 1376264 | tf_op jit(solution)/shard_map/ppermute | solution.py:17
  92.1 12.5 %collective-permute-start.7 = (bf16[16,2,7168]{2,1,0:T(2,128)(2,1)S(1)}, bf16[16,2,7168]{2,1,0:T(2,128)(2,1)S(1)}, u32[]{:S(2)}, u32[]{:S(2)}) collective-permute-start(bf16[16,2,7168]{2,1,0:T(2,128)(2,1)S(1)} %collective-permute-done.5), channel_id=1, source_target_pairs={{0,15},{1,0},{2,1},{3,2},{4,3},{5,4},{6,5},{7,6},{8,7},{9,8},{10,9... | collective-permute-start | bytes 1376264 | tf_op jit(solution)/shard_map/ppermute | solution.py:20
  102.1 15.1 %collective-permute-start.8 = (bf16[16,2,7168]{2,1,0:T(2,128)(2,1)S(1)}, bf16[16,2,7168]{2,1,0:T(2,128)(2,1)S(1)}, u32[]{:S(2)}, u32[]{:S(2)}) collective-permute-start(bf16[16,2,7168]{2,1,0:T(2,128)(2,1)S(1)} %collective-permute-done.6), channel_id=1, source_target_pairs={{0,1},{1,2},{2,3},{3,4},{4,5},{5,6},{6,7},{7,8},{8,9},{9,10},{10,1... | collective-permute-start | bytes 1376264 | tf_op jit(solution)/shard_map/ppermute | solution.py:17
  104.6 12.7 %collective-permute-start.9 = (bf16[16,2,7168]{2,1,0:T(2,128)(2,1)S(1)}, bf16[16,2,7168]{2,1,0:T(2,128)(2,1)S(1)}, u32[]{:S(2)}, u32[]{:S(2)}) collective-permute-start(bf16[16,2,7168]{2,1,0:T(2,128)(2,1)S(1)} %collective-permute-done.7), channel_id=1, source_target_pairs={{0,15},{1,0},{2,1},{3,2},{4,3},{5,4},{6,5},{7,6},{8,7},{9,8},{10,9... | collective-permute-start | bytes 1376264 | tf_op jit(solution)/shard_map/ppermute | solution.py:20
  117.1 16.9 %collective-permute-start.10 = (bf16[16,2,7168]{2,1,0:T(2,128)(2,1)S(1)}, bf16[16,2,7168]{2,1,0:T(2,128)(2,1)S(1)}, u32[]{:S(2)}, u32[]{:S(2)}) collective-permute-start(bf16[16,2,7168]{2,1,0:T(2,128)(2,1)S(1)} %collective-permute-done.8), channel_id=1, source_target_pairs={{0,1},{1,2},{2,3},{3,4},{4,5},{5,6},{6,7},{7,8},{8,9},{9,10},{10,1... | collective-permute-start | bytes 1376264 | tf_op jit(solution)/shard_map/ppermute | solution.py:17
  117.3 16.8 %collective-permute-start.11 = (bf16[16,2,7168]{2,1,0:T(2,128)(2,1)S(1)}, bf16[16,2,7168]{2,1,0:T(2,128)(2,1)S(1)}, u32[]{:S(2)}, u32[]{:S(2)}) collective-permute-start(bf16[16,2,7168]{2,1,0:T(2,128)(2,1)S(1)} %collective-permute-done.9), channel_id=1, source_target_pairs={{0,15},{1,0},{2,1},{3,2},{4,3},{5,4},{6,5},{7,6},{8,7},{9,8},{10,9... | collective-permute-start | bytes 1376264 | tf_op jit(solution)/shard_map/ppermute | solution.py:20
  134.1 15.7 %collective-permute-start.12 = (bf16[16,2,7168]{2,1,0:T(2,128)(2,1)S(1)}, bf16[16,2,7168]{2,1,0:T(2,128)(2,1)S(1)}, u32[]{:S(2)}, u32[]{:S(2)}) collective-permute-start(bf16[16,2,7168]{2,1,0:T(2,128)(2,1)S(1)} %collective-permute-done.10), channel_id=1, source_target_pairs={{0,1},{1,2},{2,3},{3,4},{4,5},{5,6},{6,7},{7,8},{8,9},{9,10},{10,1... | collective-permute-start | bytes 1376264 | tf_op jit(solution)/shard_map/ppermute | solution.py:17
  134.1 16.8 %collective-permute-start.13 = (bf16[16,2,7168]{2,1,0:T(2,128)(2,1)S(1)}, bf16[16,2,7168]{2,1,0:T(2,128)(2,1)S(1)}, u32[]{:S(2)}, u32[]{:S(2)}) collective-permute-start(bf16[16,2,7168]{2,1,0:T(2,128)(2,1)S(1)} %collective-permute-done.11), channel_id=1, source_target_pairs={{0,15},{1,0},{2,1},{3,2},{4,3},{5,4},{6,5},{7,6},{8,7},{9,8},{10,9... | collective-permute-start | bytes 1376264 | tf_op jit(solution)/shard_map/ppermute | solution.py:20
  149.8 11.5 %collective-permute-start.14 = (bf16[16,2,7168]{2,1,0:T(2,128)(2,1)S(1)}, bf16[16,2,7168]{2,1,0:T(2,128)(2,1)S(1)}, u32[]{:S(2)}, u32[]{:S(2)}) collective-permute-start(bf16[16,2,7168]{2,1,0:T(2,128)(2,1)S(1)} %collective-permute-done.12), channel_id=1, source_target_pairs={{0,1},{1,2},{2,3},{3,4},{4,5},{5,6},{6,7},{7,8},{8,9},{9,10},{10,1... | collective-permute-start | bytes 1376264 | tf_op jit(solution)/shard_map/ppermute | solution.py:17
  391.5 95.9 %copy-start.1 = (bf16[4,7168]{1,0:T(4,128)(2,1)S(1)}, bf16[4,7168]{1,0:T(4,128)(2,1)}, u32[]{:S(2)}) copy-start(bf16[4,7168]{1,0:T(4,128)(2,1)} %param.7) | copy-start | bytes 172036
Sparse Core Ops, SparseCore 0:
  398.6 86.8 reduce-scatter.3
